TPU v7x, 256 devices: a whole 4x4x8 slice. The times are simulated.
256 devices in a mesh: occi: 8 (over x_lo, y), occj: 32 (over z, x_hi, core).
Axes of the slice: x: 4 (x_hi: 2, x_lo: 2; x = x_hi * 2 + x_lo), y: 4, z: 8, core: 2. Of those that a mesh axis runs over, the one named last changes fastest.
Arguments:
- amplitudes: bfloat16 [64, 64, 256, 256], P('occi', 'occj'), may hold values from -6 to 6
- exchange: bfloat16 [64, 64, 256, 256], P('occi', 'occj'), may hold values from -6 to 6
- fock_virt: bfloat16 [256, 256], replicated, may hold values from -0.375 to 0.375
- intersection: bfloat16 [256, 256], replicated, may hold values from -0.1875 to 0.1875
- transform: bfloat16 [256, 256], replicated, may hold values from -0.375 to 0.375
- virt_energy: float32 [256], replicated, may hold values from 0.5 to 4
- occ_energy: float32 [64], replicated, may hold values from -1.5 to -0.3
- partners: int32 [64, 2], replicated, may hold values from 0 to 63, as said below
- coupling: float32 [64, 2], replicated, may hold values from -0.6 to 0.6
- domain: int32 [64, 8], replicated, may hold values 0 or 1
Outputs:
- residual: float32 [64, 64, 256, 256], P('occi', 'occj')
- new_amplitudes: bfloat16 [64, 64, 256, 256], P('occi', 'occj')
Inputs may be any that keep to these rules, and one draw needn't show every extreme that they name: The 2 partners of orbital i are distinct, differ from i, and lie within 2 of i; the first lies exactly 2 away.
All inputs are finite; a program needn't handle non-finite values.
Results may differ from a plain program's by a relative error of at most 0.0085.
Values may be sent and summed in bfloat16 or wider, within the bound.
No kernel may reach another device: no remote copies, remote signals or barrier semaphores. Data moves between devices by JAX's collectives and lax.ppermute only.
A program may use at most 128 MiB of HBM per device.

v0:
```python
import jax
import jax.numpy as jnp
from jax import lax
from jax.sharding import PartitionSpec as P

REACH = 2


def extended_2(block, sides, width):
    for axis, dim in sides:
        count = lax.axis_size(axis)
        forward = [(i, i + 1) for i in range(count - 1)]
        backward = [(target, source) for source, target in forward]
        low = lax.ppermute(
            lax.slice_in_dim(block, block.shape[dim] - width, None, axis=dim), axis, forward
        )
        high = lax.ppermute(lax.slice_in_dim(block, 0, width, axis=dim), axis, backward)
        block = jnp.concatenate([low, block, high], axis=dim)
    return block


def flip_blocks(block):
    rows_i = block.shape[0]
    cols_j = block.shape[1]
    width = block.shape[2]
    count_i = lax.axis_size("occi")
    count_j = lax.axis_size("occj")
    group = count_j // count_i
    slab = width // count_j
    moved = lax.all_to_all(
        block.reshape(1, rows_i, cols_j, width, width),
        "occj",
        split_axis=3,
        concat_axis=0,
        tiled=True,
    )
    moved = lax.all_to_all(
        moved.reshape(count_j, 1, rows_i, cols_j, slab, width),
        "occi",
        split_axis=0,
        concat_axis=1,
        tiled=True,
    )
    moved = moved.reshape(group, count_j, cols_j, cols_j, 1, slab, width)
    moved = lax.all_to_all(moved, "occj", split_axis=1, concat_axis=4, tiled=True)
    moved = moved.reshape(group, cols_j, cols_j, width, width)
    return jnp.transpose(moved, (0, 2, 1, 4, 3)).reshape(rows_i, cols_j, width, width)


def mix_rows(extended, lists, weights, start):
    local = lists - start + REACH
    total = jnp.zeros((lists.shape[0],) + extended.shape[1:], jnp.float32)
    for slot in range(lists.shape[1]):
        picked = jnp.take(extended, local[:, slot], axis=0).astype(jnp.float32)
        total = total + weights[:, slot, None, None, None] * picked
    return total


def mix_columns(extended, lists, weights, start):
    local = lists - start + REACH
    shape = (extended.shape[0], lists.shape[0]) + extended.shape[2:]
    total = jnp.zeros(shape, jnp.float32)
    for slot in range(lists.shape[1]):
        picked = jnp.take(extended, local[:, slot], axis=1).astype(jnp.float32)
        total = total + weights[None, :, slot, None, None] * picked
    return total


def per_device(
    amplitudes,
    exchange,
    fock_virt,
    intersection,
    transform,
    virt_energy,
    occ_energy,
    partners,
    coupling,
    domain,
):
    rows_i = amplitudes.shape[0]
    cols_j = amplitudes.shape[1]
    width = amplitudes.shape[2]
    tiles = domain.shape[1]
    start_i = lax.axis_index("occi") * rows_i
    start_j = lax.axis_index("occj") * cols_j
    intersection_full = (
        jnp.eye(width, dtype=jnp.float32) + intersection.astype(jnp.float32)
    ).astype(jnp.bfloat16)
    a1 = jnp.einsum(
        "ab,rsbc->rsac", fock_virt, amplitudes, preferred_element_type=jnp.float32
    ).astype(jnp.bfloat16)
    first = jnp.einsum("rsab,bc->rsac", a1, intersection_full, preferred_element_type=jnp.float32)
    a2 = jnp.einsum(
        "ab,rsbc->rsac", intersection_full, amplitudes, preferred_element_type=jnp.float32
    ).astype(jnp.bfloat16)
    second = jnp.einsum("rsab,bc->rsac", a2, fock_virt, preferred_element_type=jnp.float32)
    mirror = flip_blocks(amplitudes)
    sym = (0.5 * (amplitudes.astype(jnp.float32) + mirror.astype(jnp.float32))).astype(jnp.bfloat16)
    lists_i = lax.dynamic_slice_in_dim(partners, start_i, rows_i, 0)
    weights_i = lax.dynamic_slice_in_dim(coupling, start_i, rows_i, 0)
    extended_i = extended_2(sym, (("occi", 0),), REACH)
    c_row = mix_rows(extended_i, lists_i, weights_i, start_i).astype(jnp.bfloat16)
    lists_j = lax.dynamic_slice_in_dim(partners, start_j, cols_j, 0)
    weights_j = lax.dynamic_slice_in_dim(coupling, start_j, cols_j, 0)
    extended_j = extended_2(sym, (("occj", 1),), REACH)
    c_col = mix_columns(extended_j, lists_j, weights_j, start_j).astype(jnp.bfloat16)
    coup = c_row.astype(jnp.float32) + c_col.astype(jnp.float32)
    masks = jnp.repeat(domain.astype(jnp.float32), width // tiles, axis=1)
    mask_i = lax.dynamic_slice_in_dim(masks, start_i, rows_i, 0)
    mask_j = lax.dynamic_slice_in_dim(masks, start_j, cols_j, 0)
    mpair = jnp.maximum(mask_i[:, None, :], mask_j[None, :, :])
    two = mpair[:, :, :, None] * mpair[:, :, None, :]
    cmask = (coup * two).astype(jnp.bfloat16)
    b1 = jnp.einsum(
        "ab,rsbc->rsac", intersection_full, cmask, preferred_element_type=jnp.float32
    ).astype(jnp.bfloat16)
    third = jnp.einsum("rsab,bc->rsac", b1, intersection_full, preferred_element_type=jnp.float32)
    residual = two * (exchange.astype(jnp.float32) + first + second - third)
    resid_b = residual.astype(jnp.bfloat16)
    q1 = jnp.einsum("ba,rsbc->rsac", transform, resid_b, preferred_element_type=jnp.float32).astype(
        jnp.bfloat16
    )
    q2 = jnp.einsum("rsab,bc->rsac", q1, transform, preferred_element_type=jnp.float32)
    occ_i = lax.dynamic_slice_in_dim(occ_energy, start_i, rows_i, 0)
    occ_j = lax.dynamic_slice_in_dim(occ_energy, start_j, cols_j, 0)
    pair_shift = occ_i[:, None] + occ_j[None, :]
    denom = (
        virt_energy[None, None, :, None]
        + virt_energy[None, None, None, :]
        - pair_shift[:, :, None, None]
    )
    zeta = (q2 / denom).astype(jnp.bfloat16)
    u1 = jnp.einsum("ab,rsbc->rsac", transform, zeta, preferred_element_type=jnp.float32).astype(
        jnp.bfloat16
    )
    u2 = jnp.einsum("rsab,cb->rsac", u1, transform, preferred_element_type=jnp.float32)
    fresh = (amplitudes.astype(jnp.float32) - u2).astype(jnp.bfloat16)
    return (residual, fresh)


def solution(mesh):
    return jax.shard_map(
        per_device,
        mesh=mesh,
        in_specs=(
            P("occi", "occj", None, None),
            P("occi", "occj", None, None),
            P(),
            P(),
            P(),
            P(),
            P(),
            P(),
            P(),
            P(),
        ),
        out_specs=(P("occi", "occj", None, None), P("occi", "occj", None, None)),
        check_vma=False,
    )
```

profile of v0, /device:TPU:3, one launch (start us, length us, event | category | flops | bytes accessed | tf_op | source)
XLA Modules:
  0.0 281.1 jit_solution(13498421750724093916)
XLA Ops:
  0.6 0.0 copy-start
  0.6 3.8 %copy.94 = bf16[8,2,256,256]{3,1,0,2:T(2,128)(2,1)S(1)} copy(bf16[8,2,256,256]{3,2,1,0:T(8,128)(2,1)} %param.14) | data formatting | bytes 4194304 | tf_op args[0]
  4.4 61.2 %all_to_all.42 = bf16[1,8,2,256,256]{4,2,1,0,3:T(2,128)(2,1)S(1)} all-to-all(bf16[1,8,2,256,256]{4,2,1,0,3:T(2,128)(2,1)S(1)} %bitcast.98), channel_id=1, replica_groups=mesh['occi'=8,'occj'=32] {'occj'}, dimensions={3} | all-to-all | bytes 4194304 | tf_op jit(solution)/shard_map/all_to_all | solution.py:30
  65.6 0.7 copy.93
  66.3 0.2 copy.56
  66.6 29.6 %all_to_all.43 = bf16[32,1,8,2,8,256]{5,4,3,2,1,0:T(8,128)(2,1)S(1)} all-to-all(bf16[32,1,8,2,8,256]{5,4,3,2,1,0:T(8,128)(2,1)S(1)} %copy.56), channel_id=1, replica_groups=mesh['occi'=8,'occj'=32] {'occi'}, dimensions={0} | all-to-all | bytes 4194304 | tf_op jit(solution)/shard_map/all_to_all | solution.py:37
  96.3 0.2 copy.57
  96.5 1.5 copy.58
  98.0 0.0 copy-start.8
  98.0 0.0 copy-start.10
  98.0 0.0 copy-start.7
  98.0 0.0 copy-start.9
  98.0 7.9 %all-to-all-start.2 = ((bf16[4,32,2,2,1,8,256]{6,5,3,2,0,4,1:T(8,128)(2,1)}), bf16[4,32,2,2,1,8,256]{6,5,3,2,0,4,1:T(8,128)(2,1)S(1)}, u32[]{:S(2)}, u32[]{:S(2)}) async-start(bf16[4,32,2,2,1,8,256]{6,5,3,2,0,4,1:T(8,128)(2,1)} %copy.58), calls=%async_computation.2 | async-start | bytes 4194304 | tf_op jit(solution)/shard_map/all_to_all | solution.py:45
  105.9 0.0 copy-done.8
  106.0 0.1 constant_dynamic-slice_fusion.5
  106.1 0.1 copy.50
  106.2 0.0 copy-done.10
  106.2 0.1 dynamic_slice.30
  106.2 0.1 dynamic_slice.31
  106.3 0.1 constant_dynamic-slice_fusion.4
  106.4 0.1 copy.51
  106.5 0.0 copy-done.7
  106.5 0.1 fusion.69
  106.6 0.1 fusion.71
  106.6 0.0 copy-done.9
  106.7 0.1 constant_dynamic-slice_fusion.3
  106.7 0.1 constant_dynamic-slice_fusion.1
  106.8 0.1 broadcast_add_fusion.1
  106.9 49.1 %all-to-all-done.2 = bf16[4,32,2,2,1,8,256]{6,5,3,2,0,4,1:T(8,128)(2,1)S(1)} async-done(((bf16[4,32,2,2,1,8,256]{6,5,3,2,0,4,1:T(8,128)(2,1)}), bf16[4,32,2,2,1,8,256]{6,5,3,2,0,4,1:T(8,128)(2,1)S(1)}, u32[]{:S(2)}, u32[]{:S(2)}) %all-to-all-start.2) | async-done | bytes 2097184 | tf_op jit(solution)/shard_map/all_to_all | solution.py:45
  156.0 2.4 convert_bitcast_fusion
  158.4 0.0 copy-start.2
  158.4 5.4 %copy.60 = f32[4,2,2,256,256]{4,3,2,1,0:T(8,128)} copy(f32[4,2,2,256,256]{3,4,1,2,0:T(8,128)} %convert_bitcast_fusion) | data formatting | bytes 8388608 | tf_op jit(solution)/shard_map/convert_element_type | solution.py:99
  163.8 0.0 copy-done.2
  163.8 0.0 copy-start.6
  163.8 0.0 copy-start.3
  163.8 4.2 %fusion.1 = bf16[8,2,256,256]{3,2,1,0:T(8,128)(2,1)} fusion(bf16[8,2,256,256]{3,2,1,0:T(8,128)(2,1)S(1)} %copy-done.2, f32[4,2,2,256,256]{4,3,2,1,0:T(8,128)} %copy.60), kind=kLoop, calls=%fused_computation.10 | loop fusion | flops 4194304 | bytes 8388608 | tf_op jit(solution)/shard_map/convert_element_type | solution.py:99
  168.0 5.1 %collective-permute-start.2 = (bf16[8,2,256,256]{3,2,1,0:T(8,128)(2,1)}, bf16[8,2,256,256]{3,2,1,0:T(8,128)(2,1)}, u32[]{:S(2)}, u32[]{:S(2)}) collective-permute-start(bf16[8,2,256,256]{3,2,1,0:T(8,128)(2,1)} %fusion.1), channel_id=1, source_target_pairs={{0,1},{1,2},{2,3},{3,4},{4,5},{5,6},{6,7},{7,8},{8,9},{9,10},{10,1... | collective-permute-start | bytes 6291464 | tf_op jit(solution)/shard_map/ppermute | solution.py:14
  173.1 1.9 collective-permute-start.3
  175.1 0.0 copy-done.6
  175.1 0.8 broadcast_add_fusion
  175.9 0.0 copy-done
  175.9 0.0 copy-done.3
  175.9 4.1 %fusion.10 = f32[8,2,256,256]{3,2,1,0:T(8,128)} fusion(bf16[8,2,256,256]{3,2,1,0:T(8,128)(2,1)S(1)} %copy-done.2, bf16[256,256]{1,0:T(8,128)(2,1)S(1)} %copy-done, bf16[256,256]{1,0:T(8,128)(2,1)S(1)} %copy-done.3), kind=kOutput, calls=%fused_computation.24 | convolution fusion | flops 1075118080 | bytes 6553600 | tf_op jit(solution)/shard_map/rsab,bc->rsac/dot_general | solution.py:93
  180.0 2.3 fusion.74
  182.2 2.2 collective-permute-start
  184.4 5.4 %collective-permute-start.1 = (bf16[2,2,256,256]{3,2,1,0:T(8,128)(2,1)}, bf16[2,2,256,256]{3,2,1,0:T(8,128)(2,1)S(1)}, u32[]{:S(2)}, u32[]{:S(2)}) collective-permute-start(bf16[2,2,256,256]{3,2,1,0:T(8,128)(2,1)} %get-tuple-element.13), channel_id=1, source_target_pairs={{32,0},{64,32},{96,64},{128,96},{160,128},{192,160},{224,192},{33,... | collective-permute-start | bytes 1572872 | tf_op jit(solution)/shard_map/ppermute | solution.py:17
  189.8 3.3 %fusion.8 = f32[8,2,256,256]{3,2,1,0:T(8,128)} fusion(bf16[8,2,256,256]{3,2,1,0:T(8,128)(2,1)S(1)} %copy-done.2, bf16[256,256]{1,0:T(8,128)(2,1)S(1)} %copy-done, bf16[256,256]{1,0:T(8,128)(2,1)S(1)} %copy-done.3), kind=kOutput, calls=%fused_computation.22 | convolution fusion | flops 1075118080 | bytes 6553600 | tf_op jit(solution)/shard_map/rsab,bc->rsac/dot_general | solution.py:97
  193.1 39.3 %collective-permute-done = bf16[2,2,256,256]{3,2,1,0:T(8,128)(2,1)S(1)} collective-permute-done((bf16[2,2,256,256]{3,2,1,0:T(8,128)(2,1)}, bf16[2,2,256,256]{3,2,1,0:T(8,128)(2,1)S(1)}, u32[]{:S(2)}, u32[]{:S(2)}) %collective-permute-start) | collective-permute-done | bytes 524320 | tf_op jit(solution)/shard_map/ppermute | solution.py:14
  232.4 0.0 collective-permute-done.1
  232.4 3.0 %pad_maximum_fusion.1 = bf16[12,2,256,256]{3,2,1,0:T(8,128)(2,1)} fusion(bf16[2,2,256,256]{3,2,1,0:T(8,128)(2,1)S(1)} %collective-permute-done.1, bf16[8,2,256,256]{3,2,1,0:T(8,128)(2,1)} %fusion.1, bf16[2,2,256,256]{3,2,1,0:T(8,128)(2,1)S(1)} %collective-permute-done), kind=kLoop, calls=%fused_computation.17 | loop fusion | flops 3145728 | bytes 6291456 | tf_op jit(solution)/shard_map/concatenate | solution.py:18
  235.5 3.9 %gather_fusion = bf16[8,2,256,256]{3,2,1,0:T(8,128)(2,1)} fusion(bf16[12,2,256,256]{3,2,1,0:T(8,128)(2,1)} %pad_maximum_fusion.1, s32[1024]{0:T(1024)S(1)} %get-tuple-element.25), kind=kCustom, calls=%fused_computation.clone | custom fusion | bytes 4194336 | tf_op jit(solution)/shard_map/jit(_take)/gather | solution.py:54
  239.4 3.9 %gather_fusion.1 = bf16[8,2,256,256]{3,2,1,0:T(8,128)(2,1)} fusion(bf16[12,2,256,256]{3,2,1,0:T(8,128)(2,1)} %pad_maximum_fusion.1, s32[1024]{0:T(1024)S(1)} %get-tuple-element.24), kind=kCustom, calls=%fused_computation.2.clone | custom fusion | bytes 4194336 | tf_op jit(solution)/shard_map/jit(_take)/gather | solution.py:54
  243.3 0.0 collective-permute-done.2
  243.3 0.0 collective-permute-done.3
  243.3 6.4 %pad_maximum_fusion = bf16[8,6,256,256]{3,2,1,0:T(8,128)(2,1)} fusion(bf16[8,2,256,256]{3,2,1,0:T(8,128)(2,1)} %collective-permute-done.3, bf16[8,2,256,256]{3,2,1,0:T(8,128)(2,1)} %fusion.1, bf16[8,2,256,256]{3,2,1,0:T(8,128)(2,1)} %collective-permute-done.2), kind=kLoop, calls=%fused_computation.4 | loop fusion | flops 6291456 | bytes 12582912 | tf_op jit(solution)/shard_map/concatenate | solution.py:18
  249.7 4.8 %gather_fusion.2 = bf16[2,8,256,256]{3,2,1,0:T(8,128)(2,1)} fusion(bf16[8,6,256,256]{3,2,1,0:T(8,128)(2,1)} %pad_maximum_fusion, s32[1024]{0:T(1024)S(1)} %get-tuple-element.23), kind=kCustom, calls=%fused_computation.1.clone | custom fusion | bytes 4194312 | tf_op jit(solution)/shard_map/jit(_take)/gather | solution.py:64
  254.5 4.8 %gather_fusion.3 = bf16[2,8,256,256]{3,2,1,0:T(8,128)(2,1)} fusion(bf16[8,6,256,256]{3,2,1,0:T(8,128)(2,1)} %pad_maximum_fusion, s32[1024]{0:T(1024)S(1)} %get-tuple-element.22), kind=kCustom, calls=%fused_computation.3.clone | custom fusion | bytes 4194312 | tf_op jit(solution)/shard_map/jit(_take)/gather | solution.py:64
  259.3 0.0 copy-start.4
  259.3 10.0 %multiply_multiply_fusion = f32[8,2,256,256]{3,2,1,0:T(8,128)} fusion(f32[8,2,256,256]{3,2,1,0:T(8,128)} %fusion.8, f32[8,2,256,256]{3,2,1,0:T(8,128)} %fusion.10, bf16[8,2,256,256]{3,2,1,0:T(8,128)(2,1)} %param.15, bf16[2,8,256,256]{3,2,1,0:T(8,128)(2,1)} %gather_fusion.3, bf16[2,8,256,256]{3,2,1,0:T(8,128)(2,1)} %gather_fusion.2, ...), kind=kOutput, calls=%fused_computation.5 | convolution fusion | flops 1104805888 | bytes 23216228 | tf_op jit(solution)/shard_map/rsab,bc->rsac/dot_general | solution.py:118
  269.3 0.0 copy-done.4
  269.3 6.3 %fusion.5 = f32[8,2,256,256]{3,2,1,0:T(8,128)} fusion(f32[8,2,256,256]{3,2,1,0:T(8,128)} %multiply_multiply_fusion, bf16[256,256]{1,0:T(8,128)(2,1)S(1)} %copy-done.4), kind=kOutput, calls=%fused_computation.19 | convolution fusion | flops 1075838976 | bytes 8519680 | tf_op jit(solution)/shard_map/rsab,bc->rsac/dot_general | solution.py:124
  275.6 0.0 copy-done.5
  275.6 5.5 %fusion.2 = bf16[8,2,256,256]{3,2,1,0:T(8,128)(2,1)} fusion(bf16[8,2,256,256]{3,2,1,0:T(8,128)(2,1)S(1)} %copy-done.2, f32[8,2,256,256]{3,2,1,0:T(8,128)} %fusion.5, f32[8,2]{1,0:T(8,128)S(1)} %broadcast_add_fusion.1, f32[256,256]{1,0:T(8,128)S(1)} %copy-done.5, bf16[256,256]{1,0:T(8,128)(2,1)S(1)} %copy-done.4), kind=kOutput, calls=%fused_computation.11 | convolution fusion | flops 1081081856 | bytes 8781888 | tf_op jit(solution)/shard_map/rsab,cb->rsac/dot_general | solution.py:137
  281.1 0.0 copy-done.1
  (11 shorter events, 0.1 us)
Async XLA Ops:
  0.6 175.3 %copy-start = (bf16[256,256]{1,0:T(8,128)(2,1)S(1)}, bf16[256,256]{1,0:T(8,128)(2,1)}, u32[]{:S(2)}) copy-start(bf16[256,256]{1,0:T(8,128)(2,1)} %param.16) | copy-start | bytes 393220
  98.0 8.0 %copy-start.8 = (s32[64,8]{0,1:T(8,128)S(1)}, s32[64,8]{0,1:T(8,128)}, u32[]{:S(2)}) copy-start(s32[64,8]{0,1:T(8,128)} %param.23) | copy-start | bytes 6148
  98.0 8.2 %copy-start.10 = (f32[64]{0:T(128)S(1)}, f32[64]{0:T(128)}, u32[]{:S(2)}) copy-start(f32[64]{0:T(128)} %param.20) | copy-start | bytes 772
  98.0 8.5 %copy-start.7 = (s32[64,2]{0,1:T(2,128)S(1)}, s32[64,2]{0,1:T(2,128)}, u32[]{:S(2)}) copy-start(s32[64,2]{0,1:T(2,128)} %param.21) | copy-start | bytes 1540
  98.0 8.7 %copy-start.9 = (f32[64,2]{0,1:T(2,128)S(1)}, f32[64,2]{0,1:T(2,128)}, u32[]{:S(2)}) copy-start(f32[64,2]{0,1:T(2,128)} %param.22) | copy-start | bytes 1540
  98.0 58.0 %all-to-all-start.2 = ((bf16[4,32,2,2,1,8,256]{6,5,3,2,0,4,1:T(8,128)(2,1)}), bf16[4,32,2,2,1,8,256]{6,5,3,2,0,4,1:T(8,128)(2,1)S(1)}, u32[]{:S(2)}, u32[]{:S(2)}) async-start(bf16[4,32,2,2,1,8,256]{6,5,3,2,0,4,1:T(8,128)(2,1)} %copy.58), calls=%async_computation.2 | async-start | bytes 4194304 | tf_op jit(solution)/shard_map/all_to_all | solution.py:45
  158.4 5.4 %copy-start.2 = (bf16[8,2,256,256]{3,2,1,0:T(8,128)(2,1)S(1)}, bf16[8,2,256,256]{3,2,1,0:T(8,128)(2,1)}, u32[]{:S(2)}) copy-start(bf16[8,2,256,256]{3,2,1,0:T(8,128)(2,1)} %param.14) | copy-start | bytes 6291460
  163.8 11.3 %copy-start.6 = (f32[256]{0:T(256)S(1)}, f32[256]{0:T(256)}, u32[]{:S(2)}) copy-start(f32[256]{0:T(256)} %param.19) | copy-start | bytes 3076
  163.8 12.1 %copy-start.3 = (bf16[256,256]{1,0:T(8,128)(2,1)S(1)}, bf16[256,256]{1,0:T(8,128)(2,1)}, u32[]{:S(2)}) copy-start(bf16[256,256]{1,0:T(8,128)(2,1)} %param.17) | copy-start | bytes 393220
  168.0 75.3 %collective-permute-start.2 = (bf16[8,2,256,256]{3,2,1,0:T(8,128)(2,1)}, bf16[8,2,256,256]{3,2,1,0:T(8,128)(2,1)}, u32[]{:S(2)}, u32[]{:S(2)}) collective-permute-start(bf16[8,2,256,256]{3,2,1,0:T(8,128)(2,1)} %fusion.1), channel_id=1, source_target_pairs={{0,1},{1,2},{2,3},{3,4},{4,5},{5,6},{6,7},{7,8},{8,9},{9,10},{10,1... | collective-permute-start | bytes 6291464 | tf_op jit(solution)/shard_map/ppermute | solution.py:14
  173.1 70.2 %collective-permute-start.3 = (bf16[8,2,256,256]{3,2,1,0:T(8,128)(2,1)}, bf16[8,2,256,256]{3,2,1,0:T(8,128)(2,1)}, u32[]{:S(2)}, u32[]{:S(2)}) collective-permute-start(bf16[8,2,256,256]{3,2,1,0:T(8,128)(2,1)} %fusion.1), channel_id=1, source_target_pairs={{1,0},{2,1},{3,2},{4,3},{5,4},{6,5},{7,6},{8,7},{9,8},{10,9},{11,1... | collective-permute-start | bytes 6291464 | tf_op jit(solution)/shard_map/ppermute | solution.py:17
  182.2 50.2 %collective-permute-start = (bf16[2,2,256,256]{3,2,1,0:T(8,128)(2,1)}, bf16[2,2,256,256]{3,2,1,0:T(8,128)(2,1)S(1)}, u32[]{:S(2)}, u32[]{:S(2)}) collective-permute-start(bf16[2,2,256,256]{3,2,1,0:T(8,128)(2,1)} %get-tuple-element.12), channel_id=1, source_target_pairs={{0,32},{32,64},{64,96},{96,128},{128,160},{160,192},{192,224},{1,3... | collective-permute-start | bytes 1572872 | tf_op jit(solution)/shard_map/ppermute | solution.py:14
  184.4 48.0 %collective-permute-start.1 = (bf16[2,2,256,256]{3,2,1,0:T(8,128)(2,1)}, bf16[2,2,256,256]{3,2,1,0:T(8,128)(2,1)S(1)}, u32[]{:S(2)}, u32[]{:S(2)}) collective-permute-start(bf16[2,2,256,256]{3,2,1,0:T(8,128)(2,1)} %get-tuple-element.13), channel_id=1, source_target_pairs={{32,0},{64,32},{96,64},{128,96},{160,128},{192,160},{224,192},{33,... | collective-permute-start | bytes 1572872 | tf_op jit(solution)/shard_map/ppermute | solution.py:17
  259.3 10.0 %copy-start.4 = (bf16[256,256]{1,0:T(8,128)(2,1)S(1)}, bf16[256,256]{1,0:T(8,128)(2,1)}, u32[]{:S(2)}) copy-start(bf16[256,256]{1,0:T(8,128)(2,1)} %param.18) | copy-start | bytes 393220
  269.3 6.3 %copy-start.5 = (f32[256,256]{1,0:T(8,128)S(1)}, f32[256,256]{1,0:T(8,128)}, u32[]{:S(2)}) copy-start(f32[256,256]{1,0:T(8,128)} %broadcast_add_fusion) | copy-start | bytes 786436
  275.6 5.5 %copy-start.1 = (bf16[256,256]{1,0:T(8,128)(2,1)S(1)}, bf16[256,256]{1,0:T(8,128)(2,1)}, u32[]{:S(2)}) copy-start(bf16[256,256]{1,0:T(8,128)(2,1)} %param.16) | copy-start | bytes 393220
where the time goes:
time: 282 us; the launch traced here: 281 us
  blocking collectives  90.8 us (32%)
  waiting for transfers between devices  88.4 us (31%)
  local copies, waits for them, and re-layouts  32.2 us (11%)
  matrix products  29.2 us (10%)
  starting transfers between devices  22.5 us (8%)
  other arithmetic  17.1 us (6%)
    all_to_all x1, blocking collectives, flip_blocks(): lax.all_to_all(block.reshape(1, rows_i, cols_j, width, width), 'occj', sp...  61.2 us
    all_to_all x1, waiting for transfers between devices, flip_blocks(): lax.all_to_all(moved, 'occj', split_axis=1, concat_axis=4, tiled=True)  49.1 us
    ppermute x2, waiting for transfers between devices, extended_2(): lax.ppermute(lax.slice_in_dim(block, block.shape[dim] - width, None, axis...  39.3 us
    all_to_all x1, blocking collectives, flip_blocks(): lax.all_to_all(moved.reshape(count_j, 1, rows_i, cols_j, slab, width), 'o...  29.6 us
    dot_general x1, matrix products, per_device(): jnp.einsum('rsab,bc->rsac', b1, intersection_full, preferred_element_type...  10 us
    gather x2, local copies, waits for them, and re-layouts, mix_columns(): picked = jnp.take(extended, local[:, slot], axis=1).astype(jnp.float32)  9.58 us
    concatenate x2, other arithmetic, extended_2(): block = jnp.concatenate([low, block, high], axis=dim)  9.47 us
    all_to_all x1, starting transfers between devices, flip_blocks(): lax.all_to_all(moved, 'occj', split_axis=1, concat_axis=4, tiled=True)  7.93 us
  transfers between devices with their start and end apart: 5, of which 2 were waited for; matrix products, arithmetic and copies ran while one was open for 8% of the time, Pallas kernels for 0%

commit v1 on v0

--- a/solution.py
+++ b/solution.py
@@ -42,7 +42,10 @@
         tiled=True,
     )
     moved = moved.reshape(group, count_j, cols_j, cols_j, 1, slab, width)
-    moved = lax.all_to_all(moved, "occj", split_axis=1, concat_axis=4, tiled=True)
+    moved = jnp.concatenate(
+        lax.all_to_all(jnp.stack(jnp.split(moved, lax.axis_size("occj"), axis=1)), "occj", 0, 0),
+        axis=4,
+    )
     moved = moved.reshape(group, cols_j, cols_j, width, width)
     return jnp.transpose(moved, (0, 2, 1, 4, 3)).reshape(rows_i, cols_j, width, width)
 

time: 282 us -> 301 us (1.067)
  local copies, waits for them, and re-layouts: 32.2 us -> 50.9 us
    unnamed x23 -> x54, local copies, waits for them, and re-layouts: 3.83 us -> 23.5 us
  transfers between devices with their start and end apart: 5 -> 5, of which waited for: 2 -> 2; matrix products, arithmetic and copies ran while one was open for 8% -> 7% of each run, Pallas kernels for 0% -> 0%
where the time goes in v1:
time: 301 us; the launch traced here: 300 us
  blocking collectives  90.8 us (30%)
  waiting for transfers between devices  88.4 us (29%)
  local copies, waits for them, and re-layouts  50.9 us (17%)
  matrix products  29.2 us (10%)
  starting transfers between devices  22.5 us (7%)
  other arithmetic  17.1 us (6%)
    all_to_all x1, blocking collectives, flip_blocks(): lax.all_to_all(block.reshape(1, rows_i, cols_j, width, width), 'occj', sp...  61.2 us
    all_to_all x1, waiting for transfers between devices, flip_blocks(): lax.all_to_all(jnp.stack(jnp.split(moved, lax.axis_size('occj'), axis=1))...  49.1 us
    ppermute x2, waiting for transfers between devices, extended_2(): lax.ppermute(lax.slice_in_dim(block, block.shape[dim] - width, None, axis...  39.3 us
    all_to_all x1, blocking collectives, flip_blocks(): lax.all_to_all(moved.reshape(count_j, 1, rows_i, cols_j, slab, width), 'o...  29.6 us
    unnamed x54, local copies, waits for them, and re-layouts  23.5 us
    dot_general x1, matrix products, per_device(): jnp.einsum('rsab,bc->rsac', b1, intersection_full, preferred_element_type...  10 us
    gather x2, local copies, waits for them, and re-layouts, mix_columns(): picked = jnp.take(extended, local[:, slot], axis=1).astype(jnp.float32)  9.58 us
    concatenate x2, other arithmetic, extended_2(): block = jnp.concatenate([low, block, high], axis=dim)  9.47 us
  transfers between devices with their start and end apart: 5, of which 2 were waited for; matrix products, arithmetic and copies ran while one was open for 7% of the time, Pallas kernels for 0%

profile of v1, /device:TPU:3, one launch (start us, length us, event | category | flops | bytes accessed | tf_op | source)
XLA Modules:
  0.0 299.9 jit_solution(7278975571713075359)
XLA Ops:
  0.6 3.8 %copy.274 = bf16[8,2,256,256]{3,1,0,2:T(2,128)(2,1)S(1)} copy(bf16[8,2,256,256]{3,2,1,0:T(8,128)(2,1)} %param.14) | data formatting | bytes 4194304 | tf_op args[0]
  4.4 61.2 %all_to_all.35 = bf16[1,8,2,256,256]{4,2,1,0,3:T(2,128)(2,1)S(1)} all-to-all(bf16[1,8,2,256,256]{4,2,1,0,3:T(2,128)(2,1)S(1)} %bitcast.315), channel_id=1, replica_groups=mesh['occi'=8,'occj'=32] {'occj'}, dimensions={3} | all-to-all | bytes 4194304 | tf_op jit(solution)/shard_map/all_to_all | solution.py:30
  65.6 0.7 copy.273
  66.3 0.2 copy.177
  66.6 29.6 %all_to_all.36 = bf16[32,1,8,2,8,256]{5,4,3,2,1,0:T(8,128)(2,1)S(1)} all-to-all(bf16[32,1,8,2,8,256]{5,4,3,2,1,0:T(8,128)(2,1)S(1)} %copy.177), channel_id=1, replica_groups=mesh['occi'=8,'occj'=32] {'occi'}, dimensions={0} | all-to-all | bytes 4194304 | tf_op jit(solution)/shard_map/all_to_all | solution.py:37
  96.3 0.2 copy.178
  96.5 0.6 fusion.99
  97.1 0.6 fusion.98
  97.7 0.6 fusion.97
  98.4 0.6 fusion.96
  99.0 0.6 fusion.95
  99.6 0.6 fusion.94
  100.3 0.6 fusion.93
  100.9 0.6 fusion.92
  101.5 0.6 fusion.91
  102.2 0.6 fusion.90
  102.8 0.6 fusion.89
  103.4 0.6 fusion.88
  104.1 0.6 fusion.87
  104.7 0.6 fusion.86
  105.4 0.6 fusion.85
  106.0 0.6 fusion.84
  106.6 0.6 fusion.83
  107.3 0.6 fusion.82
  107.9 0.6 fusion.81
  108.5 0.6 fusion.80
  109.2 0.6 fusion.79
  109.8 0.6 fusion.78
  110.4 0.6 fusion.77
  111.1 0.6 fusion.76
  111.7 0.6 fusion.75
  112.3 0.6 fusion.74
  113.0 0.6 fusion.73
  113.6 0.6 fusion.72
  114.2 0.6 fusion.71
  114.9 0.6 fusion.70
  115.5 0.6 fusion.69
  116.1 0.6 fusion.68
  116.8 7.9 %all-to-all-start.2 = ((bf16[32,4,1,2,2,1,8,256]{7,6,4,3,1,5,2,0:T(8,128)(2,1)}), bf16[32,4,1,2,2,1,8,256]{7,6,4,3,1,5,2,0:T(8,128)(2,1)S(1)}, u32[]{:S(2)}, u32[]{:S(2)}) async-start(bf16[32,4,1,2,2,1,8,256]{7,6,4,3,1,5,2,0:T(8,128)(2,1)} %fusion.68), calls=%async_computation.2 | async-start | bytes 4194304 | tf_op jit(solution)/shard_map/all_to_all | solution.py:46
  124.8 0.1 constant_dynamic-slice_fusion.5
  124.9 0.1 dynamic_slice.30
  125.1 0.1 constant_dynamic-slice_fusion.4
  125.7 49.1 %all-to-all-done.2 = bf16[32,4,1,2,2,1,8,256]{7,6,4,3,1,5,2,0:T(8,128)(2,1)S(1)} async-done(((bf16[32,4,1,2,2,1,8,256]{7,6,4,3,1,5,2,0:T(8,128)(2,1)}), bf16[32,4,1,2,2,1,8,256]{7,6,4,3,1,5,2,0:T(8,128)(2,1)S(1)}, u32[]{:S(2)}, u32[]{:S(2)}) %all-to-all-start.2) | async-done | bytes 2097184 | tf_op jit(solution)/shard_map/all_to_all | solution.py:46
  174.8 2.4 copy_bitcast_fusion
  177.2 5.4 %copy.210 = f32[4,2,2,256,256]{4,3,2,1,0:T(8,128)} copy(f32[4,2,2,256,256]{3,4,1,2,0:T(8,128)} %copy_bitcast_fusion) | data formatting | bytes 8388608 | tf_op jit(solution)/shard_map/convert_element_type | solution.py:102
  182.6 4.2 %fusion.1 = bf16[8,2,256,256]{3,2,1,0:T(8,128)(2,1)} fusion(bf16[8,2,256,256]{3,2,1,0:T(8,128)(2,1)S(1)} %copy-done.2, f32[4,2,2,256,256]{4,3,2,1,0:T(8,128)} %copy.210), kind=kLoop, calls=%fused_computation.10 | loop fusion | flops 4194304 | bytes 8388608 | tf_op jit(solution)/shard_map/convert_element_type | solution.py:102
  186.7 5.1 %collective-permute-start.2 = (bf16[8,2,256,256]{3,2,1,0:T(8,128)(2,1)}, bf16[8,2,256,256]{3,2,1,0:T(8,128)(2,1)}, u32[]{:S(2)}, u32[]{:S(2)}) collective-permute-start(bf16[8,2,256,256]{3,2,1,0:T(8,128)(2,1)} %fusion.1), channel_id=1, source_target_pairs={{0,1},{1,2},{2,3},{3,4},{4,5},{5,6},{6,7},{7,8},{8,9},{9,10},{10,1... | collective-permute-start | bytes 6291464 | tf_op jit(solution)/shard_map/ppermute | solution.py:14
  191.9 1.9 collective-permute-start.3
  193.8 0.8 broadcast_add_fusion
  194.7 4.1 %fusion.10 = f32[8,2,256,256]{3,2,1,0:T(8,128)} fusion(bf16[8,2,256,256]{3,2,1,0:T(8,128)(2,1)S(1)} %copy-done.2, bf16[256,256]{1,0:T(8,128)(2,1)S(1)} %copy-done, bf16[256,256]{1,0:T(8,128)(2,1)S(1)} %copy-done.3), kind=kOutput, calls=%fused_computation.25 | convolution fusion | flops 1075118080 | bytes 6553600 | tf_op jit(solution)/shard_map/rsab,bc->rsac/dot_general | solution.py:96
  198.7 2.3 fusion.106
  201.0 2.2 collective-permute-start
  203.2 5.4 %collective-permute-start.1 = (bf16[2,2,256,256]{3,2,1,0:T(8,128)(2,1)}, bf16[2,2,256,256]{3,2,1,0:T(8,128)(2,1)S(1)}, u32[]{:S(2)}, u32[]{:S(2)}) collective-permute-start(bf16[2,2,256,256]{3,2,1,0:T(8,128)(2,1)} %get-tuple-element.13), channel_id=1, source_target_pairs={{32,0},{64,32},{96,64},{128,96},{160,128},{192,160},{224,192},{33,... | collective-permute-start | bytes 1572872 | tf_op jit(solution)/shard_map/ppermute | solution.py:17
  208.6 3.3 %fusion.8 = f32[8,2,256,256]{3,2,1,0:T(8,128)} fusion(bf16[8,2,256,256]{3,2,1,0:T(8,128)(2,1)S(1)} %copy-done.2, bf16[256,256]{1,0:T(8,128)(2,1)S(1)} %copy-done, bf16[256,256]{1,0:T(8,128)(2,1)S(1)} %copy-done.3), kind=kOutput, calls=%fused_computation.23 | convolution fusion | flops 1075118080 | bytes 6553600 | tf_op jit(solution)/shard_map/rsab,bc->rsac/dot_general | solution.py:100
  211.9 39.3 %collective-permute-done = bf16[2,2,256,256]{3,2,1,0:T(8,128)(2,1)S(1)} collective-permute-done((bf16[2,2,256,256]{3,2,1,0:T(8,128)(2,1)}, bf16[2,2,256,256]{3,2,1,0:T(8,128)(2,1)S(1)}, u32[]{:S(2)}, u32[]{:S(2)}) %collective-permute-start) | collective-permute-done | bytes 524320 | tf_op jit(solution)/shard_map/ppermute | solution.py:14
  251.2 3.0 %pad_maximum_fusion.1 = bf16[12,2,256,256]{3,2,1,0:T(8,128)(2,1)} fusion(bf16[2,2,256,256]{3,2,1,0:T(8,128)(2,1)S(1)} %collective-permute-done.1, bf16[8,2,256,256]{3,2,1,0:T(8,128)(2,1)} %fusion.1, bf16[2,2,256,256]{3,2,1,0:T(8,128)(2,1)S(1)} %collective-permute-done), kind=kLoop, calls=%fused_computation.18 | loop fusion | flops 3145728 | bytes 6291456 | tf_op jit(solution)/shard_map/concatenate | solution.py:18
  254.2 3.9 %gather_fusion = bf16[8,2,256,256]{3,2,1,0:T(8,128)(2,1)} fusion(bf16[12,2,256,256]{3,2,1,0:T(8,128)(2,1)} %pad_maximum_fusion.1, s32[1024]{0:T(1024)S(1)} %get-tuple-element.25), kind=kCustom, calls=%fused_computation.clone | custom fusion | bytes 4194336 | tf_op jit(solution)/shard_map/jit(_take)/gather | solution.py:57
  258.1 3.9 %gather_fusion.1 = bf16[8,2,256,256]{3,2,1,0:T(8,128)(2,1)} fusion(bf16[12,2,256,256]{3,2,1,0:T(8,128)(2,1)} %pad_maximum_fusion.1, s32[1024]{0:T(1024)S(1)} %get-tuple-element.24), kind=kCustom, calls=%fused_computation.2.clone | custom fusion | bytes 4194336 | tf_op jit(solution)/shard_map/jit(_take)/gather | solution.py:57
  262.0 6.4 %pad_maximum_fusion = bf16[8,6,256,256]{3,2,1,0:T(8,128)(2,1)} fusion(bf16[8,2,256,256]{3,2,1,0:T(8,128)(2,1)} %collective-permute-done.3, bf16[8,2,256,256]{3,2,1,0:T(8,128)(2,1)} %fusion.1, bf16[8,2,256,256]{3,2,1,0:T(8,128)(2,1)} %collective-permute-done.2), kind=kLoop, calls=%fused_computation.4 | loop fusion | flops 6291456 | bytes 12582912 | tf_op jit(solution)/shard_map/concatenate | solution.py:18
  268.5 4.8 %gather_fusion.2 = bf16[2,8,256,256]{3,2,1,0:T(8,128)(2,1)} fusion(bf16[8,6,256,256]{3,2,1,0:T(8,128)(2,1)} %pad_maximum_fusion, s32[1024]{0:T(1024)S(1)} %get-tuple-element.23), kind=kCustom, calls=%fused_computation.1.clone | custom fusion | bytes 4194312 | tf_op jit(solution)/shard_map/jit(_take)/gather | solution.py:67
  273.3 4.8 %gather_fusion.3 = bf16[2,8,256,256]{3,2,1,0:T(8,128)(2,1)} fusion(bf16[8,6,256,256]{3,2,1,0:T(8,128)(2,1)} %pad_maximum_fusion, s32[1024]{0:T(1024)S(1)} %get-tuple-element.22), kind=kCustom, calls=%fused_computation.3.clone | custom fusion | bytes 4194312 | tf_op jit(solution)/shard_map/jit(_take)/gather | solution.py:67
  278.0 10.0 %multiply_multiply_fusion = f32[8,2,256,256]{3,2,1,0:T(8,128)} fusion(f32[8,2,256,256]{3,2,1,0:T(8,128)} %fusion.8, f32[8,2,256,256]{3,2,1,0:T(8,128)} %fusion.10, bf16[8,2,256,256]{3,2,1,0:T(8,128)(2,1)} %param.15, bf16[2,8,256,256]{3,2,1,0:T(8,128)(2,1)} %gather_fusion.3, bf16[2,8,256,256]{3,2,1,0:T(8,128)(2,1)} %gather_fusion.2, ...), kind=kOutput, calls=%fused_computation.5 | convolution fusion | flops 1104805888 | bytes 23216228 | tf_op jit(solution)/shard_map/rsab,bc->rsac/dot_general | solution.py:121
  288.1 6.3 %fusion.5 = f32[8,2,256,256]{3,2,1,0:T(8,128)} fusion(f32[8,2,256,256]{3,2,1,0:T(8,128)} %multiply_multiply_fusion, bf16[256,256]{1,0:T(8,128)(2,1)S(1)} %copy-done.4), kind=kOutput, calls=%fused_computation.20 | convolution fusion | flops 1075838976 | bytes 8519680 | tf_op jit(solution)/shard_map/rsab,bc->rsac/dot_general | solution.py:127
  294.4 5.5 %fusion.2 = bf16[8,2,256,256]{3,2,1,0:T(8,128)(2,1)} fusion(bf16[8,2,256,256]{3,2,1,0:T(8,128)(2,1)S(1)} %copy-done.2, f32[8,2,256,256]{3,2,1,0:T(8,128)} %fusion.5, f32[8,2]{1,0:T(8,128)S(1)} %broadcast_add_fusion.1, f32[256,256]{1,0:T(8,128)S(1)} %copy-done.5, bf16[256,256]{1,0:T(8,128)(2,1)S(1)} %copy-done.4), kind=kOutput, calls=%fused_computation.11 | convolution fusion | flops 1081081856 | bytes 8781888 | tf_op jit(solution)/shard_map/rsab,cb->rsac/dot_general | solution.py:140
  (42 shorter events, 0.7 us)
Async XLA Ops:
  0.6 194.0 %copy-start = (bf16[256,256]{1,0:T(8,128)(2,1)S(1)}, bf16[256,256]{1,0:T(8,128)(2,1)}, u32[]{:S(2)}) copy-start(bf16[256,256]{1,0:T(8,128)(2,1)} %param.16) | copy-start | bytes 393220
  116.8 8.0 %copy-start.8 = (s32[64,8]{0,1:T(8,128)S(1)}, s32[64,8]{0,1:T(8,128)}, u32[]{:S(2)}) copy-start(s32[64,8]{0,1:T(8,128)} %param.23) | copy-start | bytes 6148
  116.8 8.2 %copy-start.10 = (f32[64]{0:T(128)S(1)}, f32[64]{0:T(128)}, u32[]{:S(2)}) copy-start(f32[64]{0:T(128)} %param.20) | copy-start | bytes 772
  116.8 8.5 %copy-start.7 = (s32[64,2]{0,1:T(2,128)S(1)}, s32[64,2]{0,1:T(2,128)}, u32[]{:S(2)}) copy-start(s32[64,2]{0,1:T(2,128)} %param.21) | copy-start | bytes 1540
  116.8 8.7 %copy-start.9 = (f32[64,2]{0,1:T(2,128)S(1)}, f32[64,2]{0,1:T(2,128)}, u32[]{:S(2)}) copy-start(f32[64,2]{0,1:T(2,128)} %param.22) | copy-start | bytes 1540
  116.8 58.0 %all-to-all-start.2 = ((bf16[32,4,1,2,2,1,8,256]{7,6,4,3,1,5,2,0:T(8,128)(2,1)}), bf16[32,4,1,2,2,1,8,256]{7,6,4,3,1,5,2,0:T(8,128)(2,1)S(1)}, u32[]{:S(2)}, u32[]{:S(2)}) async-start(bf16[32,4,1,2,2,1,8,256]{7,6,4,3,1,5,2,0:T(8,128)(2,1)} %fusion.68), calls=%async_computation.2 | async-start | bytes 4194304 | tf_op jit(solution)/shard_map/all_to_all | solution.py:46
  177.2 5.4 %copy-start.2 = (bf16[8,2,256,256]{3,2,1,0:T(8,128)(2,1)S(1)}, bf16[8,2,256,256]{3,2,1,0:T(8,128)(2,1)}, u32[]{:S(2)}) copy-start(bf16[8,2,256,256]{3,2,1,0:T(8,128)(2,1)} %param.14) | copy-start | bytes 6291460
  182.6 11.3 %copy-start.6 = (f32[256]{0:T(256)S(1)}, f32[256]{0:T(256)}, u32[]{:S(2)}) copy-start(f32[256]{0:T(256)} %param.19) | copy-start | bytes 3076
  182.6 12.1 %copy-start.3 = (bf16[256,256]{1,0:T(8,128)(2,1)S(1)}, bf16[256,256]{1,0:T(8,128)(2,1)}, u32[]{:S(2)}) copy-start(bf16[256,256]{1,0:T(8,128)(2,1)} %param.17) | copy-start | bytes 393220
  186.7 75.3 %collective-permute-start.2 = (bf16[8,2,256,256]{3,2,1,0:T(8,128)(2,1)}, bf16[8,2,256,256]{3,2,1,0:T(8,128)(2,1)}, u32[]{:S(2)}, u32[]{:S(2)}) collective-permute-start(bf16[8,2,256,256]{3,2,1,0:T(8,128)(2,1)} %fusion.1), channel_id=1, source_target_pairs={{0,1},{1,2},{2,3},{3,4},{4,5},{5,6},{6,7},{7,8},{8,9},{9,10},{10,1... | collective-permute-start | bytes 6291464 | tf_op jit(solution)/shard_map/ppermute | solution.py:14
  191.9 70.2 %collective-permute-start.3 = (bf16[8,2,256,256]{3,2,1,0:T(8,128)(2,1)}, bf16[8,2,256,256]{3,2,1,0:T(8,128)(2,1)}, u32[]{:S(2)}, u32[]{:S(2)}) collective-permute-start(bf16[8,2,256,256]{3,2,1,0:T(8,128)(2,1)} %fusion.1), channel_id=1, source_target_pairs={{1,0},{2,1},{3,2},{4,3},{5,4},{6,5},{7,6},{8,7},{9,8},{10,9},{11,1... | collective-permute-start | bytes 6291464 | tf_op jit(solution)/shard_map/ppermute | solution.py:17
  201.0 50.2 %collective-permute-start = (bf16[2,2,256,256]{3,2,1,0:T(8,128)(2,1)}, bf16[2,2,256,256]{3,2,1,0:T(8,128)(2,1)S(1)}, u32[]{:S(2)}, u32[]{:S(2)}) collective-permute-start(bf16[2,2,256,256]{3,2,1,0:T(8,128)(2,1)} %get-tuple-element.12), channel_id=1, source_target_pairs={{0,32},{32,64},{64,96},{96,128},{128,160},{160,192},{192,224},{1,3... | collective-permute-start | bytes 1572872 | tf_op jit(solution)/shard_map/ppermute | solution.py:14
  203.2 48.0 %collective-permute-start.1 = (bf16[2,2,256,256]{3,2,1,0:T(8,128)(2,1)}, bf16[2,2,256,256]{3,2,1,0:T(8,128)(2,1)S(1)}, u32[]{:S(2)}, u32[]{:S(2)}) collective-permute-start(bf16[2,2,256,256]{3,2,1,0:T(8,128)(2,1)} %get-tuple-element.13), channel_id=1, source_target_pairs={{32,0},{64,32},{96,64},{128,96},{160,128},{192,160},{224,192},{33,... | collective-permute-start | bytes 1572872 | tf_op jit(solution)/shard_map/ppermute | solution.py:17
  278.0 10.0 %copy-start.4 = (bf16[256,256]{1,0:T(8,128)(2,1)S(1)}, bf16[256,256]{1,0:T(8,128)(2,1)}, u32[]{:S(2)}) copy-start(bf16[256,256]{1,0:T(8,128)(2,1)} %param.18) | copy-start | bytes 393220
  288.1 6.3 %copy-start.5 = (f32[256,256]{1,0:T(8,128)S(1)}, f32[256,256]{1,0:T(8,128)}, u32[]{:S(2)}) copy-start(f32[256,256]{1,0:T(8,128)} %broadcast_add_fusion) | copy-start | bytes 786436
  294.4 5.5 %copy-start.1 = (bf16[256,256]{1,0:T(8,128)(2,1)S(1)}, bf16[256,256]{1,0:T(8,128)(2,1)}, u32[]{:S(2)}) copy-start(bf16[256,256]{1,0:T(8,128)(2,1)} %param.16) | copy-start | bytes 393220
